TPU v7x, 32 devices: a whole 2x2x4 slice. The times are simulated.
32 devices in a mesh: shot: 8 (over z, y), surf: 4 (over x, core).
Axes of the slice: x: 2, y: 2, z: 4, core: 2. Of those that a mesh axis runs over, the one named last changes fastest.
Arguments:
- traces: bfloat16 [64, 1024, 2048], P('shot', 'surf'), may hold values from -6 to 6
- rec_point: int32 [1024], P('surf'), may hold values from 0 to 1023, as said below
- plan: int32 [8], replicated, may hold values from 0 to 7, each once
- green_blocks: bfloat16 [2, 32, 1024, 1024], P(None, 'shot', 'surf'), may hold values from -0.1875 to 0.1875
Outputs:
- multiples: float32 [2, 16, 64, 1024], P(None, None, 'shot', 'surf')
Inputs may be any that keep to these rules, and one draw needn't show every extreme that they name: `plan`: each block index appears once; the first 4 entries are used. `rec_point`: receiver r and its surface point p lie in the same one of the equal groups of 256 receivers and 256 surface points, counted in order: p // 256 == r // 256.
All inputs are finite; a program needn't handle non-finite values.
Results may differ from a plain program's by a relative error of at most 0.0029.
Values may be sent and summed in bfloat16 or wider, within the bound.
A program may use at most 128 MiB of HBM per device.

v0:
```python
import jax
import jax.numpy as jnp
from jax import lax
from jax.sharding import PartitionSpec as P

T_SIZE = 2048
FB = 4
STEPS = 4
FREQS = 16


def spread(value, axis, source):
    kept = jnp.where(lax.axis_index(axis) == source, value, 0).astype(value.dtype)
    return lax.psum(kept, axis)


def fourier_basis_table(freq_bins):
    times = jnp.arange(T_SIZE, dtype=jnp.int32)
    phases = freq_bins[None, :] * times[:, None] % T_SIZE
    angles = phases.astype(jnp.float32) * (2.0 * jnp.pi / T_SIZE)
    scaling = 1.0 / jnp.sqrt(jnp.float32(T_SIZE))
    return jnp.concatenate([jnp.cos(angles), -jnp.sin(angles)], axis=1) * scaling


def complex_product(spectra_part, green_part):

    def spectral_product(left_operand, right_operand):
        return jnp.einsum(
            "pwy,pyb->pwb", left_operand, right_operand, preferred_element_type=jnp.float32
        )

    real_part = spectral_product(spectra_part[0], green_part[0]) - spectral_product(
        spectra_part[1], green_part[1]
    )
    imag_part = spectral_product(spectra_part[0], green_part[1]) + spectral_product(
        spectra_part[1], green_part[0]
    )
    return jnp.stack([real_part, imag_part])


def body(traces, rec_point, plan, green_blocks):
    source_shot_count = traces.shape[0]
    point_count = green_blocks.shape[2]
    first_point = lax.axis_index("surf") * point_count
    local_point = rec_point - first_point
    onehot = (local_point[:, None] == jnp.arange(point_count, dtype=jnp.int32)[None, :]).astype(
        jnp.bfloat16
    )
    binned = jnp.einsum("rx,srt->sxt", onehot, traces, preferred_element_type=jnp.float32)
    blocks = plan[:STEPS]
    frequency_band_rows = (blocks[:, None] * FB + jnp.arange(FB, dtype=jnp.int32)[None, :]).reshape(
        -1
    )
    table = fourier_basis_table(frequency_band_rows + 4)
    flat = jnp.dot(
        binned.reshape(source_shot_count * point_count, T_SIZE),
        table,
        precision=lax.Precision.HIGHEST,
    )
    spectra = flat.astype(jnp.bfloat16).reshape(source_shot_count, point_count, 2, FREQS)
    spectra = jnp.transpose(spectra, (2, 3, 0, 1))
    multiple_outputs = []
    for number in range(STEPS):
        owner = blocks[number]
        received = spread(green_blocks, "shot", owner)
        spectra_part = spectra[:, number * FB : (number + 1) * FB]
        partial_value = complex_product(spectra_part, received)
        multiple_outputs.append(
            lax.psum_scatter(partial_value, "surf", scatter_dimension=3, tiled=True)
        )
    return jnp.concatenate(multiple_outputs, axis=1)


def solution(mesh):
    in_specs = (P("shot", "surf", None), P("surf"), P(), P(None, "shot", "surf", None))
    out_specs = P(None, None, "shot", "surf")
    return jax.shard_map(body, mesh=mesh, in_specs=in_specs, out_specs=out_specs, check_vma=False)
```

profile of v0, /device:TPU:0, one launch (start us, length us, event | category | flops | bytes accessed | tf_op | source)
XLA Modules:
  0.0 637.2 jit_solution(2940348707855232743)
XLA Ops:
  6.5 1.5 fusion.48
  10.5 7.4 %broadcast_select_fusion.3 = (bf16[2,4,256,1024]{3,2,1,0:T(8,128)(2,1)}, bf16[2,4,256,1024]{3,2,1,0:T(8,128)(2,1)}, bf16[2,4,256,1024]{3,2,1,0:T(8,128)(2,1)}, bf16[2,4,256,1024]{3,2,1,0:T(8,128)(2,1)}) fusion(bf16[2,4,256,1024]{3,2,1,0:T(8,128)(2,1)} %param.7, pred[]{:T(512)S(6)} %eq.30, pred[]{:T(512)S(6)} %eq.31, pred[]{:T(512)S(6)} %eq.33, pred[]{:T(512)S(6)} %eq.32), kind=kLoop, calls=%fused_computation.3 | loop fusion | flops 8388608 | bytes 20971524 | tf_op jit(solution)/shard_map/jit(_where)/select_n | solution.py:13
  19.4 5.7 fusion.35
  25.1 15.7 %convolution_convert_fusion = bf16[2048,32]{0,1:T(8,128)(2,1)S(1)} fusion(f32[2048,2048]{1,0:T(8,128)S(1)} %bitcast.131, f32[2048,16]{0,1:T(8,128)S(1)} %get-tuple-element.14, f32[2048,16]{0,1:T(8,128)S(1)} %get-tuple-element.13), kind=kOutput, calls=%fused_computation.4 | convolution fusion | flops 1610809344 | bytes 17170432 | tf_op jit(solution)/shard_map/dot_general | solution.py:55
  40.8 492.6 %all-reduce.3.cloned.1.call-done = (bf16[2,4,256,1024]{3,2,1,0:T(8,128)(2,1)}, bf16[2,4,256,1024]{3,2,1,0:T(8,128)(2,1)}, bf16[2,4,256,1024]{3,2,1,0:T(8,128)(2,1)}, bf16[2,4,256,1024]{3,2,1,0:T(8,128)(2,1)}) async-done(((bf16[2,4,256,1024]{3,2,1,0:T(8,128)(2,1)}, bf16[2,4,256,1024]{3,2,1,0:T(8,128)(2,1)}, bf16[2,4,256,1024]{3,2,1,0:T(8,128)(2,1)}, bf16[2,4,256,1024]{3,2,1,0:T(8,128)(2,1)}), ...) | async-done | bytes 16777232 | tf_op jit(solution)/shard_map/psum | solution.py:14
  533.4 2.1 fusion.12
  535.5 2.7 fusion.13
  539.8 0.6 copy-done
  541.6 0.7 pad_maximum_fusion.3
  542.4 2.0 fusion.21
  544.4 0.8 pad_maximum_fusion.2
  545.2 2.0 fusion.5
  547.1 2.0 fusion.25
  549.2 0.7 pad_maximum_fusion.1
  550.0 2.0 fusion
  551.9 2.0 fusion.1
  554.0 2.0 fusion.31
  556.0 2.0 fusion.29
  558.0 0.7 pad_maximum_fusion
  558.7 2.7 reduce-scatter.11.cloned.1.call-done
  561.4 22.6 %reduce-scatter.9.cloned.1.call-done = f32[2,4,8,256]{3,2,1,0:T(8,128)} async-done(((f32[2,4,8,1024]{3,2,1,0:T(8,128)}), f32[2,4,8,256]{3,2,1,0:T(8,128)}) %reduce-scatter.9.cloned.1.call-update) | async-done | bytes 65552 | tf_op jit(solution)/shard_map/reduce_scatter | solution.py:69
  584.1 22.4 %reduce-scatter.7.cloned.1.call-done = f32[2,4,8,256]{3,2,1,0:T(8,128)} async-done(((f32[2,4,8,1024]{3,2,1,0:T(8,128)}), f32[2,4,8,256]{3,2,1,0:T(8,128)}) %reduce-scatter.7.cloned.1.call-update) | async-done | bytes 65552 | tf_op jit(solution)/shard_map/reduce_scatter | solution.py:69
  606.5 22.5 %reduce-scatter.5.cloned.1.call-done = f32[2,4,8,256]{3,2,1,0:T(8,128)} async-done(((f32[2,4,8,1024]{3,2,1,0:T(8,128)}), f32[2,4,8,256]{3,2,1,0:T(8,128)}) %reduce-scatter.5.cloned.1.call-update) | async-done | bytes 65552 | tf_op jit(solution)/shard_map/reduce_scatter | solution.py:69
  629.0 1.7 pad_maximum_fusion.4
  (32 shorter events, 4.3 us)
Async XLA Ops:
  6.5 526.9 %all-reduce.3.cloned.1.call-start = ((), (), s32[]{:S(2)}) async-start(), calls=%async_computation.8 | async-start | bytes 33554432 | tf_op jit(solution)/shard_map/psum | solution.py:14
  18.0 0.7 copy-start.3
  18.0 0.8 copy-start.4
  18.0 543.4 %reduce-scatter.11.cloned.1.call-start = ((), (), s32[]{:S(2)}) async-start(), calls=%async_computation.7 | async-start | bytes 327680 | tf_op jit(solution)/shard_map/reduce_scatter | solution.py:69
  533.4 4.9 copy-start.1
  533.4 5.6 copy-start.2
  538.3 2.2 copy-start
  542.4 41.7 %reduce-scatter.9.cloned.1.call-start = ((), (), s32[]{:S(2)}) async-start(), calls=%async_computation.6 | async-start | bytes 327680 | tf_op jit(solution)/shard_map/reduce_scatter | solution.py:69
  549.2 57.3 %reduce-scatter.7.cloned.1.call-start = ((), (), s32[]{:S(2)}) async-start(), calls=%async_computation.5 | async-start | bytes 327680 | tf_op jit(solution)/shard_map/reduce_scatter | solution.py:69
  553.9 75.0 %reduce-scatter.5.cloned.1.call-start = ((), (), s32[]{:S(2)}) async-start(), calls=%async_computation.4 | async-start | bytes 327680 | tf_op jit(solution)/shard_map/reduce_scatter | solution.py:69
Sparse Core Ops, SparseCore 0:
  18.1 515.2 all-reduce.2
  542.5 18.9 reduce-scatter.10
  564.0 19.9 reduce-scatter.8
  586.4 20.0 reduce-scatter.6
  608.9 19.9 reduce-scatter.4
where the time goes:
time: 638 us; the launch traced here: 637 us
  waiting for transfers between devices  563 us (88%)
  matrix products  42.8 us (7%)
  between operations  15.7 us (2%)
  other arithmetic  12.7 us (2%)
    psum x1, waiting for transfers between devices, spread(): return lax.psum(kept, axis)  493 us
    reduce_scatter x4, waiting for transfers between devices, body(): lax.psum_scatter(partial_value, 'surf', scatter_dimension=3, tiled=True)  70.2 us
    dot_general x16, matrix products, spectral_product(): jnp.einsum('pwy,pyb->pwb', left_operand, right_operand, preferred_element...  21.4 us
    dot_general x1, matrix products, body(): jnp.dot(binned.reshape(source_shot_count * point_count, T_SIZE), table, p...  15.7 us
  transfers between devices with their start and end apart: 5, of which 5 were waited for; matrix products, arithmetic and copies ran while one was open for 6% of the time, Pallas kernels for 0%

commit v1 on v0

v1 whole, which is shorter than its diff:
```python
import functools

import jax
import jax.numpy as jnp
import numpy as np
from jax import lax
from jax.experimental import pallas as pl
from jax.experimental.pallas import tpu as pltpu
from jax.sharding import PartitionSpec as P

T_SIZE = 2048
FB = 4
STEPS = 4
FIRST_BIN = 4


def basis_table(block_count):
    bins = FIRST_BIN + np.arange(block_count * FB)
    phases = (bins[None, :] * np.arange(T_SIZE)[:, None]) % T_SIZE
    angles = phases * (2.0 * np.pi / T_SIZE)
    table = np.stack([np.cos(angles), -np.sin(angles)], axis=2) / np.sqrt(T_SIZE)
    table = table.reshape(T_SIZE, -1).astype(np.float32)
    high = table.astype(jnp.bfloat16)
    low = (table - high.astype(np.float32)).astype(jnp.bfloat16)
    return np.concatenate([high, low], axis=1)


def kernel(
    n_shot, n_surf,
    plan_ref, rec_ref, table_hbm, traces_hbm, green_hbm,
    out_ref,
    table, traces, green, spec32, outgoing, incoming,
    part, core_in, half_out, half_in, ret_out, ret_in,
    load_sem, trace_sem, fwd_send, fwd_recv, core_send, core_recv,
    surf_send, surf_recv, ret_send, ret_recv,
):
    me = lax.axis_index("shot")
    surf = lax.axis_index("surf")
    core = lax.rem(surf, 2)
    row = surf // 2
    n_rows = n_surf // 2
    shots, r_dev, _ = traces.shape
    x_dev = green.shape[2]
    cols = spec32.shape[1]
    mesh_id = pl.DeviceIdType.MESH

    load_table = pltpu.make_async_copy(table_hbm, table, load_sem.at[0])
    load_table.start()
    for s in range(shots):
        pltpu.make_async_copy(traces_hbm.at[s], traces.at[s], trace_sem.at[s]).start()
    load_green = pltpu.make_async_copy(green_hbm, green, load_sem.at[1])
    load_green.start()

    barrier = pltpu.get_barrier_semaphore()
    for d in range(1, n_shot):
        pl.semaphore_signal(
            barrier, inc=1, device_id=(lax.rem(me + d, n_shot), surf), device_id_type=mesh_id
        )
    pl.semaphore_signal(
        barrier, inc=1, device_id=(me, row * 2 + 1 - core), device_id_type=mesh_id
    )
    for d in range(1, n_rows):
        pl.semaphore_signal(
            barrier, inc=1, device_id=(me, lax.rem(row + d, n_rows) * 2 + core),
            device_id_type=mesh_id,
        )

    local = rec_ref[...] - surf * x_dev
    hot = (lax.broadcasted_iota(jnp.int32, (x_dev, r_dev), 0) == local).astype(jnp.float32)
    hot = hot.astype(jnp.bfloat16)
    load_table.wait()

    def one_shot(s, carry):
        pltpu.make_async_copy(traces_hbm.at[s], traces.at[s], trace_sem.at[s]).wait()
        both = jnp.dot(traces[s], table[...], preferred_element_type=jnp.float32).T
        value = both[:cols] + both[cols:]
        high = value.astype(jnp.bfloat16)
        low = (value - high.astype(jnp.float32)).astype(jnp.bfloat16)
        split = jnp.concatenate([high, low], axis=0)
        moved = lax.dot_general(
            split, hot, (((1,), (1,)), ((), ())), preferred_element_type=jnp.float32
        )
        spec32[s] = moved[:cols] + moved[cols:]
        return carry

    lax.fori_loop(0, shots, one_shot, 0)
    outgoing[...] = jnp.swapaxes(spec32[...], 0, 1).reshape(outgoing.shape).astype(jnp.bfloat16)

    pl.semaphore_wait(barrier, (n_shot - 1) + 1 + (n_rows - 1))

    sends = []
    forward = []
    for d in range(1, n_shot):
        to = lax.rem(me + d, n_shot)
        copy = pltpu.make_async_remote_copy(
            outgoing.at[to], incoming.at[me], fwd_send.at[d], fwd_recv.at[d],
            device_id=(to, surf), device_id_type=mesh_id,
        )
        copy.start()
        forward.append(copy)
    incoming[me] = outgoing[me]
    load_green.wait()
    for copy in forward:
        copy.wait_recv()
    sends += forward

    core_copies, surf_copies, ret_copies = {}, {}, []
    block = 2 * shots

    def multiply(j):
        values = incoming[:, j * block:(j + 1) * block, :].reshape(n_shot * block, x_dev)
        for q in range(n_surf):
            span = slice(q * r_dev, (q + 1) * r_dev)
            by_re = jnp.dot(values, green[0, j, :, span], preferred_element_type=jnp.float32)
            by_im = jnp.dot(values, green[1, j, :, span], preferred_element_type=jnp.float32)
            by_re = by_re.reshape(n_shot, 2, shots, r_dev)
            by_im = by_im.reshape(n_shot, 2, shots, r_dev)
            part[j, q % 2, q // 2, :, 0] = by_re[:, 0] - by_im[:, 1]
            part[j, q % 2, q // 2, :, 1] = by_im[:, 0] + by_re[:, 1]
        copy = pltpu.make_async_remote_copy(
            part.at[j, 1 - core], core_in.at[j], core_send.at[j], core_recv.at[j],
            device_id=(me, row * 2 + 1 - core), device_id_type=mesh_id,
        )
        copy.start()
        core_copies[j] = copy

    def cross(j):
        core_copies[j].wait_recv()
        surf_copies[j] = []
        for d in range(1, n_rows):
            to = lax.rem(row + d, n_rows)
            total = part[j, core, to] + core_in[j, to]
            half_out[j, d - 1] = total.reshape(n_shot, block, r_dev).astype(jnp.bfloat16)
            copy = pltpu.make_async_remote_copy(
                half_out.at[j, d - 1], half_in.at[j, d - 1],
                surf_send.at[j, d - 1], surf_recv.at[j, d - 1],
                device_id=(me, to * 2 + core), device_id_type=mesh_id,
            )
            copy.start()
            surf_copies[j].append(copy)

    def give_back(j):
        total = (part[j, core, row] + core_in[j, row]).reshape(n_shot, block, r_dev)
        for d in range(1, n_rows):
            surf_copies[j][d - 1].wait_recv()
            total = total + half_in[j, d - 1].astype(jnp.float32)
        ret_out[j] = total.astype(jnp.bfloat16)
        for d in range(1, n_shot):
            to = lax.rem(me + d, n_shot)
            copy = pltpu.make_async_remote_copy(
                ret_out.at[j, to], ret_in.at[j, me],
                ret_send.at[j, d], ret_recv.at[j, d],
                device_id=(to, surf), device_id_type=mesh_id,
            )
            copy.start()
            ret_copies.append(copy)
        ret_in[j, me] = ret_out[j, me]

    for t in range(FB + 2):
        if t < FB:
            multiply(t)
        if 0 <= t - 1 < FB:
            cross(t - 1)
        if 0 <= t - 2 < FB:
            give_back(t - 2)

    for copy in ret_copies:
        copy.wait_recv()
    for k in range(STEPS):
        chosen = plan_ref[k]
        for j in range(FB):
            value = ret_in[j, chosen].astype(jnp.float32)
            out_ref[0, k * FB + j] = value[:shots]
            out_ref[1, k * FB + j] = value[shots:]

    for copy in sends:
        copy.wait_send()
    for j in range(FB):
        core_copies[j].wait_send()
        for copy in surf_copies[j]:
            copy.wait_send()
    for copy in ret_copies:
        copy.wait_send()


def solution(mesh):
    n_shot, n_surf = mesh.shape["shot"], mesh.shape["surf"]
    n_rows = n_surf // 2
    table = basis_table(n_shot)

    def body(traces, rec_point, plan, green):
        shots, r_dev, _ = traces.shape
        x_dev = green.shape[2]
        block = 2 * shots
        cols = n_shot * FB * 2
        bf16, f32 = jnp.bfloat16, jnp.float32
        dma = pltpu.SemaphoreType.DMA
        whole = pl.BlockSpec(memory_space=pl.ANY)
        return pl.pallas_call(
            functools.partial(kernel, n_shot, n_surf),
            out_shape=jax.ShapeDtypeStruct((2, STEPS * FB, shots, r_dev), f32),
            in_specs=[
                pl.BlockSpec(memory_space=pltpu.SMEM),
                pl.BlockSpec(memory_space=pltpu.VMEM),
                whole, whole, whole,
            ],
            out_specs=pl.BlockSpec(memory_space=pltpu.VMEM),
            scratch_shapes=[
                pltpu.VMEM(table.shape, bf16),
                pltpu.VMEM(traces.shape, bf16),
                pltpu.VMEM(green.shape, bf16),
                pltpu.VMEM((shots, cols, x_dev), f32),
                pltpu.VMEM((n_shot, FB * block, x_dev), bf16),
                pltpu.VMEM((n_shot, FB * block, x_dev), bf16),
                pltpu.VMEM((FB, 2, n_rows, n_shot, 2, shots, r_dev), f32),
                pltpu.VMEM((FB, n_rows, n_shot, 2, shots, r_dev), f32),
                pltpu.VMEM((FB, n_rows - 1, n_shot, block, r_dev), bf16),
                pltpu.VMEM((FB, n_rows - 1, n_shot, block, r_dev), bf16),
                pltpu.VMEM((FB, n_shot, block, r_dev), bf16),
                pltpu.VMEM((FB, n_shot, block, r_dev), bf16),
                dma((2,)),
                dma((shots,)),
                dma((n_shot,)), dma((n_shot,)),
                dma((FB,)), dma((FB,)),
                dma((FB, n_rows)), dma((FB, n_rows)),
                dma((FB, n_shot)), dma((FB, n_shot)),
            ],
            compiler_params=pltpu.CompilerParams(
                collective_id=0, has_side_effects=True, vmem_limit_bytes=48 << 20
            ),
        )(plan, rec_point.reshape(1, r_dev), jnp.asarray(table), traces, green)

    in_specs = (P("shot", "surf", None), P("surf"), P(), P(None, "shot", "surf", None))
    out_specs = P(None, None, "shot", "surf")
    return jax.shard_map(body, mesh=mesh, in_specs=in_specs, out_specs=out_specs, check_vma=False)
```

time: 638 us -> 37.9 us (0.06)
  waiting for transfers between devices: 563 us -> 0 us
  matrix products: 42.8 us -> 0 us
  Pallas kernels: 0 us -> 32.4 us
  between operations: 15.7 us -> 0.01 us
  other arithmetic: 12.7 us -> 0 us
    psum x1 -> x0, waiting for transfers between devices: 493 us -> none  [spread(): return lax.psum(kept, axis)]
    reduce_scatter x4 -> x0, waiting for transfers between devices: 70.2 us -> none  [body(): lax.psum_scatter(partial_value, 'surf', scatter_dimension=3, tiled=True)]
    dot_general x18 -> x0, matrix products: 42.8 us -> none  [the longest x16 21.4 us: spectral_product(): jnp.einsum('pwy,pyb->pwb', left_operand, right_operand, preferred_element...]
    pallas_call x0 -> x1, Pallas kernels: none -> 32.4 us  [body(): pl.pallas_call(functools.partial(kernel, n_shot, n_surf), out_shape=jax.S...]
    select_n x1 -> x0, other arithmetic: 7.43 us -> none  [spread(): jnp.where(lax.axis_index(axis) == source, value, 0).astype(value.dtype)]
  transfers between devices with their start and end apart: 5 -> 0, of which waited for: 5 -> 0; matrix products, arithmetic and copies ran while one was open for 6% -> 0% of each run, Pallas kernels for 0% -> 0%
where the time goes in v1:
time: 37.9 us; the launch traced here: 37.6 us
  Pallas kernels  32.4 us (85%)
  local copies, waits for them, and re-layouts  5.27 us (14%)
    pallas_call x1, Pallas kernels, body(): pl.pallas_call(functools.partial(kernel, n_shot, n_surf), out_shape=jax.S...  32.4 us
    unnamed x9, local copies, waits for them, and re-layouts  5.27 us

profile of v1, /device:TPU:0, one launch (start us, length us, event | category | flops | bytes accessed | tf_op | source)
XLA Modules:
  0.0 37.6 jit_solution(16410669512075913551)
XLA Ops:
  0.0 0.0 copy-start
  0.0 2.2 %copy-done = bf16[2,4,256,1024]{3,2,1,0:T(8,128)(2,1)S(1)} copy-done((bf16[2,4,256,1024]{3,2,1,0:T(8,128)(2,1)S(1)}, bf16[2,4,256,1024]{3,2,1,0:T(8,128)(2,1)}, u32[]{:S(2)}) %copy-start) | copy-done | bytes 4194328
  2.2 0.0 copy-start.1
  2.2 1.0 %copy-done.1 = bf16[2048,128]{1,0:T(8,128)(2,1)S(1)} copy-done((bf16[2048,128]{1,0:T(8,128)(2,1)S(1)}, bf16[2048,128]{1,0:T(8,128)(2,1)}, u32[]{:S(2)}) %copy-start.1) | copy-done | bytes 524312
  3.2 0.0 copy-start.2
  3.2 0.7 %copy-done.2 = s32[256]{0:T(256)S(1)} copy-done((s32[256]{0:T(256)S(1)}, s32[256]{0:T(256)}, u32[]{:S(2)}) %copy-start.2) | copy-done | bytes 1048
  3.9 0.0 copy-start.3
  3.9 0.7 %copy-done.3 = s32[8]{0:T(128)S(1)} copy-done((s32[8]{0:T(128)S(1)}, s32[8]{0:T(128)}, u32[]{:S(2)}) %copy-start.3) | copy-done | bytes 56
  4.6 32.4 %shard_map.55 = f32[2,16,8,256]{3,2,1,0:T(8,128)S(1)} custom-call(s32[8]{0:T(128)S(1)} %copy-done.3, s32[1,256]{1,0:T(1,128)S(1)} %bitcast.1, bf16[2048,128]{1,0:T(8,128)(2,1)S(1)} %copy-done.1, bf16[8,256,2048]{2,1,0:T(8,128)(2,1)} %traces_hbm.1, bf16[2,4,256,1024]{3,2,1,0:T(8,128)(2,1)S(1)} %copy-done), custom_call_target="tpu_custom_call" | custom-call | tf_op jit(solution)/shard_map/pallas_call | solution.py:199
  36.9 0.7 %copy.7 = f32[2,16,8,256]{3,2,1,0:T(8,128)} copy(f32[2,16,8,256]{3,2,1,0:T(8,128)S(1)} %shard_map.55) | data formatting | bytes 524288
Async XLA Ops:
  0.0 2.2 %copy-start = (bf16[2,4,256,1024]{3,2,1,0:T(8,128)(2,1)S(1)}, bf16[2,4,256,1024]{3,2,1,0:T(8,128)(2,1)}, u32[]{:S(2)}) copy-start(bf16[2,4,256,1024]{3,2,1,0:T(8,128)(2,1)} %green_hbm.1) | copy-start | bytes 12582916
  2.2 1.0 %copy-start.1 = (bf16[2048,128]{1,0:T(8,128)(2,1)S(1)}, bf16[2048,128]{1,0:T(8,128)(2,1)}, u32[]{:S(2)}) copy-start(bf16[2048,128]{1,0:T(8,128)(2,1)} %constant.2.clone.table_hbm) | copy-start | bytes 1572868
  3.2 0.7 %copy-start.2 = (s32[256]{0:T(256)S(1)}, s32[256]{0:T(256)}, u32[]{:S(2)}) copy-start(s32[256]{0:T(256)} %param.6) | copy-start | bytes 3076
  3.9 0.7 %copy-start.3 = (s32[8]{0:T(128)S(1)}, s32[8]{0:T(128)}, u32[]{:S(2)}) copy-start(s32[8]{0:T(128)} %plan_ref.1) | copy-start | bytes 100

commit v2 on v1

--- a/solution.py
+++ b/solution.py
@@ -12,6 +12,8 @@
 FB = 4
 STEPS = 4
 FIRST_BIN = 4
+CHUNKS = 4
+SKEW = 3
 
 
 def basis_table(block_count):
@@ -27,9 +29,9 @@
 
 def kernel(
     n_shot, n_surf,
-    plan_ref, rec_ref, table_hbm, traces_hbm, green_hbm,
+    plan_hbm, rec_hbm, table_hbm, traces_hbm, green_hbm,
     out_ref,
-    table, traces, green, spec32, outgoing, incoming,
+    plan_ref, rec_ref, table, traces, green, spec32, outgoing, incoming,
     part, core_in, half_out, half_in, ret_out, ret_in,
     load_sem, trace_sem, fwd_send, fwd_recv, core_send, core_recv,
     surf_send, surf_recv, ret_send, ret_recv,
@@ -45,11 +47,15 @@
     mesh_id = pl.DeviceIdType.MESH
 
     load_table = pltpu.make_async_copy(table_hbm, table, load_sem.at[0])
+    load_rec = pltpu.make_async_copy(rec_hbm, rec_ref, load_sem.at[2])
+    load_rec.start()
     load_table.start()
     for s in range(shots):
         pltpu.make_async_copy(traces_hbm.at[s], traces.at[s], trace_sem.at[s]).start()
     load_green = pltpu.make_async_copy(green_hbm, green, load_sem.at[1])
     load_green.start()
+    load_plan = pltpu.make_async_copy(plan_hbm, plan_ref, load_sem.at[3])
+    load_plan.start()
 
     barrier = pltpu.get_barrier_semaphore()
     for d in range(1, n_shot):
@@ -65,6 +71,7 @@
             device_id_type=mesh_id,
         )
 
+    load_rec.wait()
     local = rec_ref[...] - surf * x_dev
     hot = (lax.broadcasted_iota(jnp.int32, (x_dev, r_dev), 0) == local).astype(jnp.float32)
     hot = hot.astype(jnp.bfloat16)
@@ -88,26 +95,30 @@
 
     pl.semaphore_wait(barrier, (n_shot - 1) + 1 + (n_rows - 1))
 
-    sends = []
-    forward = []
-    for d in range(1, n_shot):
-        to = lax.rem(me + d, n_shot)
-        copy = pltpu.make_async_remote_copy(
-            outgoing.at[to], incoming.at[me], fwd_send.at[d], fwd_recv.at[d],
-            device_id=(to, surf), device_id_type=mesh_id,
-        )
-        copy.start()
-        forward.append(copy)
+    block = 2 * shots
+    width = FB // CHUNKS
+    order = sorted(range(1, n_shot), key=lambda d: abs(2 * d - n_shot))
+    forward = {}
+    for c in range(CHUNKS):
+        rows = pl.ds(c * width * block, width * block)
+        for d in order:
+            to = lax.rem(me + d, n_shot)
+            copy = pltpu.make_async_remote_copy(
+                outgoing.at[to, rows], incoming.at[me, rows],
+                fwd_send.at[c, d], fwd_recv.at[c, d],
+                device_id=(to, surf), device_id_type=mesh_id,
+            )
+            copy.start()
+            forward[c, d] = copy
     incoming[me] = outgoing[me]
     load_green.wait()
-    for copy in forward:
-        copy.wait_recv()
-    sends += forward
 
     core_copies, surf_copies, ret_copies = {}, {}, []
-    block = 2 * shots
 
     def multiply(j):
+        if j % width == 0:
+            for d in order:
+                forward[j // width, d].wait_recv()
         values = incoming[:, j * block:(j + 1) * block, :].reshape(n_shot * block, x_dev)
         for q in range(n_surf):
             span = slice(q * r_dev, (q + 1) * r_dev)
@@ -145,7 +156,7 @@
             surf_copies[j][d - 1].wait_recv()
             total = total + half_in[j, d - 1].astype(jnp.float32)
         ret_out[j] = total.astype(jnp.bfloat16)
-        for d in range(1, n_shot):
+        for d in order:
             to = lax.rem(me + d, n_shot)
             copy = pltpu.make_async_remote_copy(
                 ret_out.at[j, to], ret_in.at[j, me],
@@ -156,16 +167,17 @@
             ret_copies.append(copy)
         ret_in[j, me] = ret_out[j, me]
 
-    for t in range(FB + 2):
+    for t in range(FB + SKEW):
         if t < FB:
             multiply(t)
         if 0 <= t - 1 < FB:
             cross(t - 1)
-        if 0 <= t - 2 < FB:
-            give_back(t - 2)
+        if 0 <= t - SKEW < FB:
+            give_back(t - SKEW)
 
     for copy in ret_copies:
         copy.wait_recv()
+    load_plan.wait()
     for k in range(STEPS):
         chosen = plan_ref[k]
         for j in range(FB):
@@ -173,7 +185,7 @@
             out_ref[0, k * FB + j] = value[:shots]
             out_ref[1, k * FB + j] = value[shots:]
 
-    for copy in sends:
+    for copy in forward.values():
         copy.wait_send()
     for j in range(FB):
         core_copies[j].wait_send()
@@ -195,17 +207,15 @@
         cols = n_shot * FB * 2
         bf16, f32 = jnp.bfloat16, jnp.float32
         dma = pltpu.SemaphoreType.DMA
-        whole = pl.BlockSpec(memory_space=pl.ANY)
+        whole = pl.BlockSpec(memory_space=pltpu.HBM)
         return pl.pallas_call(
             functools.partial(kernel, n_shot, n_surf),
             out_shape=jax.ShapeDtypeStruct((2, STEPS * FB, shots, r_dev), f32),
-            in_specs=[
-                pl.BlockSpec(memory_space=pltpu.SMEM),
-                pl.BlockSpec(memory_space=pltpu.VMEM),
-                whole, whole, whole,
-            ],
+            in_specs=[whole] * 5,
             out_specs=pl.BlockSpec(memory_space=pltpu.VMEM),
             scratch_shapes=[
+                pltpu.SMEM(plan.shape, jnp.int32),
+                pltpu.VMEM((1, r_dev), jnp.int32),
                 pltpu.VMEM(table.shape, bf16),
                 pltpu.VMEM(traces.shape, bf16),
                 pltpu.VMEM(green.shape, bf16),
@@ -218,15 +228,15 @@
                 pltpu.VMEM((FB, n_rows - 1, n_shot, block, r_dev), bf16),
                 pltpu.VMEM((FB, n_shot, block, r_dev), bf16),
                 pltpu.VMEM((FB, n_shot, block, r_dev), bf16),
-                dma((2,)),
+                dma((4,)),
                 dma((shots,)),
-                dma((n_shot,)), dma((n_shot,)),
+                dma((CHUNKS, n_shot)), dma((CHUNKS, n_shot)),
                 dma((FB,)), dma((FB,)),
                 dma((FB, n_rows)), dma((FB, n_rows)),
                 dma((FB, n_shot)), dma((FB, n_shot)),
             ],
             compiler_params=pltpu.CompilerParams(
-                collective_id=0, has_side_effects=True, vmem_limit_bytes=48 << 20
+                collective_id=0, has_side_effects=True, vmem_limit_bytes=60 << 20
             ),
         )(plan, rec_point.reshape(1, r_dev), jnp.asarray(table), traces, green)
 

time: 37.9 us -> 33.6 us (0.89)
  local copies, waits for them, and re-layouts: 5.27 us -> 1.67 us
  Pallas kernels: 32.4 us -> 31.8 us
    unnamed x9 -> x1, local copies, waits for them, and re-layouts: 5.27 us -> 1.67 us
    pallas_call x1, Pallas kernels: 32.4 us -> 31.8 us  [body(): pl.pallas_call(functools.partial(kernel, n_shot, n_surf), out_shape=jax.S...]
where the time goes in v2:
time: 33.6 us; the launch traced here: 33.5 us
  Pallas kernels  31.8 us (95%)
  local copies, waits for them, and re-layouts  1.67 us (5%)
    pallas_call x1, Pallas kernels, body(): pl.pallas_call(functools.partial(kernel, n_shot, n_surf), out_shape=jax.S...  31.8 us
    unnamed x1, local copies, waits for them, and re-layouts  1.67 us

profile of v2, /device:TPU:0, one launch (start us, length us, event | category | flops | bytes accessed | tf_op | source)
XLA Modules:
  0.0 33.5 jit_solution(5989807393128322319)
XLA Ops:
  0.0 31.8 %shard_map.55 = f32[2,16,8,256]{3,2,1,0:T(8,128)} custom-call(s32[8]{0:T(128)} %plan_hbm.1, s32[1,256]{1,0:T(1,128)} %bitcast.1, bf16[2048,128]{1,0:T(8,128)(2,1)} %constant.2.clone.table_hbm, bf16[8,256,2048]{2,1,0:T(8,128)(2,1)} %traces_hbm.1, bf16[2,4,256,1024]{3,2,1,0:T(8,128)(2,1)} %green_hbm.1), custom_call_target="tpu_custom_call" | custom-call | tf_op jit(solution)/shard_map/pallas_call | solution.py:211
  31.8 1.7 %copy.7 = f32[2,16,8,256]{3,2,1,0:T(8,128)} copy(f32[2,16,8,256]{3,2,1,0:T(8,128)} %shard_map.55) | data formatting | bytes 524288

commit v3 on v2

--- a/solution.py
+++ b/solution.py
@@ -46,19 +46,9 @@
     cols = spec32.shape[1]
     mesh_id = pl.DeviceIdType.MESH
 
-    load_table = pltpu.make_async_copy(table_hbm, table, load_sem.at[0])
-    load_rec = pltpu.make_async_copy(rec_hbm, rec_ref, load_sem.at[2])
-    load_rec.start()
-    load_table.start()
-    for s in range(shots):
-        pltpu.make_async_copy(traces_hbm.at[s], traces.at[s], trace_sem.at[s]).start()
-    load_green = pltpu.make_async_copy(green_hbm, green, load_sem.at[1])
-    load_green.start()
-    load_plan = pltpu.make_async_copy(plan_hbm, plan_ref, load_sem.at[3])
-    load_plan.start()
-
+    order = sorted(range(1, n_shot), key=lambda d: abs(2 * d - n_shot))
     barrier = pltpu.get_barrier_semaphore()
-    for d in range(1, n_shot):
+    for d in order:
         pl.semaphore_signal(
             barrier, inc=1, device_id=(lax.rem(me + d, n_shot), surf), device_id_type=mesh_id
         )
@@ -71,6 +61,16 @@
             device_id_type=mesh_id,
         )
 
+    load_table = pltpu.make_async_copy(table_hbm, table, load_sem.at[0])
+    load_rec = pltpu.make_async_copy(rec_hbm, rec_ref, load_sem.at[2])
+    load_rec.start()
+    load_table.start()
+    for s in range(3):
+        pltpu.make_async_copy(traces_hbm.at[s], traces.at[s], trace_sem.at[s]).start()
+    load_green = pltpu.make_async_copy(green_hbm, green, load_sem.at[1])
+    load_plan = pltpu.make_async_copy(plan_hbm, plan_ref, load_sem.at[3])
+    load_plan.start()
+
     load_rec.wait()
     local = rec_ref[...] - surf * x_dev
     hot = (lax.broadcasted_iota(jnp.int32, (x_dev, r_dev), 0) == local).astype(jnp.float32)
@@ -79,6 +79,10 @@
 
     def one_shot(s, carry):
         pltpu.make_async_copy(traces_hbm.at[s], traces.at[s], trace_sem.at[s]).wait()
+        if s + 3 < shots:
+            pltpu.make_async_copy(traces_hbm.at[s + 3], traces.at[s + 3], trace_sem.at[s + 3]).start()
+        elif s + 3 == shots:
+            load_green.start()
         both = jnp.dot(traces[s], table[...], preferred_element_type=jnp.float32).T
         value = both[:cols] + both[cols:]
         high = value.astype(jnp.bfloat16)
@@ -90,14 +94,14 @@
         spec32[s] = moved[:cols] + moved[cols:]
         return carry
 
-    lax.fori_loop(0, shots, one_shot, 0)
+    for s in range(shots):
+        one_shot(s, 0)
     outgoing[...] = jnp.swapaxes(spec32[...], 0, 1).reshape(outgoing.shape).astype(jnp.bfloat16)
 
     pl.semaphore_wait(barrier, (n_shot - 1) + 1 + (n_rows - 1))
 
     block = 2 * shots
     width = FB // CHUNKS
-    order = sorted(range(1, n_shot), key=lambda d: abs(2 * d - n_shot))
     forward = {}
     for c in range(CHUNKS):
         rows = pl.ds(c * width * block, width * block)
@@ -181,9 +185,7 @@
     for k in range(STEPS):
         chosen = plan_ref[k]
         for j in range(FB):
-            value = ret_in[j, chosen].astype(jnp.float32)
-            out_ref[0, k * FB + j] = value[:shots]
-            out_ref[1, k * FB + j] = value[shots:]
+            out_ref[k * FB + j] = ret_in[j, chosen]
 
     for copy in forward.values():
         copy.wait_send()
@@ -208,9 +210,9 @@
         bf16, f32 = jnp.bfloat16, jnp.float32
         dma = pltpu.SemaphoreType.DMA
         whole = pl.BlockSpec(memory_space=pltpu.HBM)
-        return pl.pallas_call(
+        chosen = pl.pallas_call(
             functools.partial(kernel, n_shot, n_surf),
-            out_shape=jax.ShapeDtypeStruct((2, STEPS * FB, shots, r_dev), f32),
+            out_shape=jax.ShapeDtypeStruct((STEPS * FB, block, r_dev), bf16),
             in_specs=[whole] * 5,
             out_specs=pl.BlockSpec(memory_space=pltpu.VMEM),
             scratch_shapes=[
@@ -236,9 +238,11 @@
                 dma((FB, n_shot)), dma((FB, n_shot)),
             ],
             compiler_params=pltpu.CompilerParams(
-                collective_id=0, has_side_effects=True, vmem_limit_bytes=60 << 20
+                collective_id=0, has_side_effects=True, vmem_limit_bytes=48 << 20
             ),
-        )(plan, rec_point.reshape(1, r_dev), jnp.asarray(table), traces, green)
+        )(*[pltpu.with_memory_space_constraint(v, pltpu.HBM) for v in (plan, rec_point.reshape(1, r_dev), jnp.asarray(table), traces, green)])
+        chosen = chosen.reshape(STEPS * FB, 2, shots, r_dev).astype(f32)
+        return jnp.swapaxes(chosen, 0, 1)
 
     in_specs = (P("shot", "surf", None), P("surf"), P(), P(None, "shot", "surf", None))
     out_specs = P(None, None, "shot", "surf")

time: 33.6 us -> 30.5 us (0.908)
  Pallas kernels: 31.8 us -> 29.6 us
  local copies, waits for them, and re-layouts: 1.67 us -> 0 us
  other arithmetic: 0 us -> 0.72 us
    pallas_call x1, Pallas kernels: 31.8 us -> 29.6 us  [body(): pl.pallas_call(functools.partial(kernel, n_shot, n_surf), out_shape=jax.S...]
    unnamed x1 -> x0, local copies, waits for them, and re-layouts: 1.67 us -> none
    transpose x0 -> x1, other arithmetic: none -> 0.72 us  [body(): return jnp.swapaxes(chosen, 0, 1)]
where the time goes in v3:
time: 30.5 us; the launch traced here: 30.3 us
  Pallas kernels  29.6 us (97%)
  other arithmetic  0.72 us (2%)
    pallas_call x1, Pallas kernels, body(): pl.pallas_call(functools.partial(kernel, n_shot, n_surf), out_shape=jax.S...  29.6 us
    transpose x1, other arithmetic, body(): return jnp.swapaxes(chosen, 0, 1)  0.72 us

profile of v3, /device:TPU:0, one launch (start us, length us, event | category | flops | bytes accessed | tf_op | source)
XLA Modules:
  0.0 30.3 jit_solution(5221358094291692137)
XLA Ops:
  0.0 29.6 %shard_map.55 = bf16[16,16,256]{2,1,0:T(8,128)(2,1)S(1)} custom-call(s32[8]{0:T(128)} %plan_hbm.1, s32[1,256]{1,0:T(1,128)} %bitcast.7, bf16[2048,128]{1,0:T(8,128)(2,1)} %constant.2.clone.table_hbm, bf16[8,256,2048]{2,1,0:T(8,128)(2,1)} %traces_hbm.1, bf16[2,4,256,1024]{3,2,1,0:T(8,128)(2,1)} %green_hbm.1), custom_call_target="tpu_custom_call" | custom-call | tf_op jit(solution)/shard_map/pallas_call | solution.py:213
  29.6 0.7 %copy_bitcast_fusion = f32[2,16,8,256]{3,2,1,0:T(8,128)} fusion(bf16[16,16,256]{2,1,0:T(8,128)(2,1)S(1)} %shard_map.55), kind=kLoop, calls=%fused_computation | loop fusion | flops 65536 | bytes 393216 | tf_op jit(solution)/shard_map/transpose | solution.py:245
